TPU v7x, 256 devices: a whole 4x4x8 slice. The times are simulated.
256 devices in a mesh: patch: 4 (over x), line: 16 (over z, core), layer: 4 (over y).
Axes of the slice: x: 4, y: 4, z: 8, core: 2. Of those that a mesh axis runs over, the one named last changes fastest.
Arguments:
- elastic: float32 [4, 5, 1024, 2048], P('patch', None, 'line', 'layer'), may hold values from -6 to 6
- acoustic: float32 [4, 3, 1024, 2048], P('patch', None, 'line', 'layer'), may hold values from -6 to 6
- el_media: float32 [4, 3, 1024, 2048], P('patch', None, 'line', 'layer'), may hold values from 0.2 to 1.5
- ac_media: float32 [4, 2, 1024, 2048], P('patch', None, 'line', 'layer'), may hold values from 0.2 to 1.5
- cont_matrix: float32 [128, 20], replicated, may hold values from -1.25 to 1.25
- fringe_cells: int32 [4, 16, 4, 4, 256], P('patch', 'line', 'layer'), may hold values from 0 to 32767, as said below
- donor_cells: int32 [4, 16, 4, 4, 4, 256], P('patch', 'line', 'layer'), may hold values from 0 to 32767
- donor_weights: float32 [4, 16, 4, 4, 4, 256], P('patch', 'line', 'layer'), may hold values from 0 to 1, as said below
- donor_counts: int32 [4, 16, 4, 4], P('patch', 'line', 'layer'), may hold values from 0 to 256, as said below
- el_pair: int32 [4, 1024], P('patch', 'line'), may hold values from 0 to 63
- ac_pair: int32 [4, 1024], P('patch', 'line'), may hold values from 0 to 63
Outputs:
- new_elastic: float32 [4, 5, 1024, 2048], P('patch', None, 'line', 'layer')
- new_acoustic: float32 [4, 3, 1024, 2048], P('patch', None, 'line', 'layer')
Inputs may be any that keep to these rules, and one draw needn't show every extreme that they name: `fringe_cells`: within one device the 1024 fringe cells are distinct. `donor_weights`: Positive; the four weights of a slot sum to 1. `donor_counts`: 0 where donor and receiver are the same patch; on every device one donor patch fills all 256 slots.
All inputs are finite; a program needn't handle non-finite values.
Results may differ from a plain program's by a relative error of at most 0.0001.
Values sent between devices are 32-bit elements; how exact they have to be, the bound alone decides.
A program may use at most 128 MiB of HBM per device.

v0:
```python
import functools
import math

import jax
import jax.numpy as jnp
import numpy as np
from jax import lax
from jax.experimental import pallas as pl
from jax.experimental.pallas import tpu as pltpu
from jax.sharding import PartitionSpec as P

P_SIZE = 1152
MATCH = 10
NF = 8
NQ = 4
SL = 64
LANES = 128
MESH_ID = pl.DeviceIdType.MESH
F32 = jnp.float32
BF16 = jnp.bfloat16

EL_OF = {0: 0, 1: 1, 2: 2, 3: 4, 6: 3}
AC_OF = {4: 0, 5: 1, 7: 2}
FED = {0: (2, 6), 1: (3,), 2: (0,), 3: (1,), 4: (5,), 5: (4,)}


def derivative_rows():
    d = np.arange(128)[:, None] - (np.arange(2048)[None, :] - 896)
    d = d % P_SIZE
    angle = np.where(d == 0, 1.0, np.pi * d / P_SIZE)
    value = np.where(d == 0, 0.0, (np.pi / P_SIZE) * np.where(d % 2 == 0, 1.0, -1.0) / np.tan(angle))
    high = value.astype(np.float32).astype(jnp.bfloat16)
    low = (value - high.astype(np.float64)).astype(np.float32).astype(jnp.bfloat16)
    return np.stack([high, low])


def halves(x):
    high = x.astype(BF16)
    low = (x - high.astype(F32)).astype(BF16)
    return high, low


def dot(a, b):
    return jnp.dot(a, b, preferred_element_type=F32)


def exact_dot(a, b):
    return jnp.dot(a, b, preferred_element_type=F32, precision=lax.Precision.HIGHEST)


def lanes_of(shape):
    return lax.broadcasted_iota(jnp.int32, shape, len(shape) - 1)


def rows_of(shape):
    return lax.broadcasted_iota(jnp.int32, shape, len(shape) - 2)


def kernel(
    cnt, el, ac, em, am, cm, fc, dc, dw, elp, acp, wt,
    oel, oac,
    F, H, XF, XP, XB, E, YA, YB, DA, DB, W, CM, FC, PAIR, MEL, MAC,
    RC, RW, VS, VR, S, TH, TL, OH, ACC, SC, MK, HP, HN, O, CO,
    s_load, s_med, s_small, s_fa, r_fa, s_fb, r_fb, s_ra, r_ra, s_rb, r_rb,
    s_rc, r_rc, s_rw, r_rw, s_v, r_v, s_h, r_h, s_out,
):
    me = lax.axis_index("line")
    zc = me // 2
    core = me % 2
    pt = lax.axis_index("patch")
    ly = lax.axis_index("layer")

    def line_of(dz, k):
        return ((zc + dz + 8) % 8) * 2 + k

    loads = {}
    for f in range(NF):
        for q in range(NQ):
            src = el.at[0, EL_OF[f], :, pl.ds(q * LANES, LANES)] if f in EL_OF else ac.at[0, AC_OF[f], :, pl.ds(q * LANES, LANES)]
            loads[f, q] = pltpu.make_async_copy(src, F.at[f, q], s_load.at[f * NQ + q])
            loads[f, q].start()
    small = [
        pltpu.make_async_copy(wt, W, s_small.at[0]),
        pltpu.make_async_copy(cm, CM, s_small.at[1]),
        pltpu.make_async_copy(fc.at[0, 0, 0], FC, s_small.at[2]),
        pltpu.make_async_copy(elp, PAIR.at[0], s_small.at[3]),
        pltpu.make_async_copy(acp, PAIR.at[1], s_small.at[4]),
    ]
    for c in small:
        c.start()
    media = []
    for f in range(3):
        for q in range(NQ):
            media.append(pltpu.make_async_copy(em.at[0, f, :, pl.ds(q * LANES, LANES)], MEL.at[f, q], s_med.at[f * NQ + q]))
    for f in range(2):
        for q in range(NQ):
            media.append(pltpu.make_async_copy(am.at[0, f, :, pl.ds(q * LANES, LANES)], MAC.at[f, q], s_med.at[12 + f * NQ + q]))

    barrier = pltpu.get_barrier_semaphore()
    partners = [{"line": (me + o) % 16} for o in range(1, 16)]
    partners += [{"patch": (pt + o) % 4} for o in range(1, 4)]
    partners += [{"layer": (ly + o) % 4} for o in (1, 3)]
    for p in partners:
        pl.semaphore_signal(barrier, inc=1, device_id=p, device_id_type=MESH_ID)

    for f in range(6):
        for q in range(NQ):
            loads[f, q].wait()
    left64 = lanes_of((32, LANES)) < 64
    for c in range(8):
        t = 3 * c + 1
        top = F[t // 4, t % 4, 0:32]
        bot = F[t // 4, t % 4, 32:64]
        H[2 * c] = jnp.where(left64, top, pltpu.roll(bot, 64, 1))
        H[2 * c + 1] = jnp.where(left64, pltpu.roll(top, 64, 1), bot)
    for f in range(6, 8):
        for q in range(NQ):
            loads[f, q].wait()

    pl.semaphore_wait(barrier, len(partners))

    reqs = []
    for o in range(1, 4):
        q = (pt + o) % 4
        reqs.append(pltpu.make_async_remote_copy(
            src_ref=dc.at[0, 0, 0, q], dst_ref=RC.at[o - 1], send_sem=s_rc.at[o - 1], recv_sem=r_rc.at[o - 1],
            device_id={"patch": q}, device_id_type=MESH_ID))
        reqs.append(pltpu.make_async_remote_copy(
            src_ref=dw.at[0, 0, 0, q], dst_ref=RW.at[o - 1], send_sem=s_rw.at[o - 1], recv_sem=r_rw.at[o - 1],
            device_id={"patch": q}, device_id_type=MESH_ID))
    for r in reqs:
        r.start()
    halo_up = pltpu.make_async_remote_copy(
        src_ref=F.at[:, 0], dst_ref=HN, send_sem=s_h.at[0], recv_sem=r_h.at[0],
        device_id={"layer": (ly + 3) % 4}, device_id_type=MESH_ID)
    halo_down = pltpu.make_async_remote_copy(
        src_ref=F.at[:, 3], dst_ref=HP, send_sem=s_h.at[1], recv_sem=r_h.at[1],
        device_id={"layer": (ly + 1) % 4}, device_id_type=MESH_ID)
    halo_up.start()
    halo_down.start()

    order = [(dz, k) for dz in (4, 3, -3, 2, -2, 1, -1) for k in (0, 1)]
    n_out = len(order)
    other = 1 - core

    def targets():
        for i, (dz, k) in enumerate(order):
            kk = k if i % 2 == k else k
            yield i, (zc + dz + 8) % 8, kk
        yield n_out, zc, other

    def exchange(src_of, dst, send, recv):
        copies = []
        for i, c, k in targets():
            copies.append(pltpu.make_async_remote_copy(
                src_ref=src_of(c, k), dst_ref=dst.at[me], send_sem=send.at[i], recv_sem=recv.at[me],
                device_id={"line": c * 2 + k}, device_id_type=MESH_ID))
        own = pltpu.make_async_copy(src_of(zc, core), dst.at[me], recv.at[me])
        for r in copies:
            r.start()
        own.start()
        return copies

    def full_tile(c, k):
        t = 3 * c + 2 * k
        return F.at[t // 4, t % 4]

    fwd_a = exchange(full_tile, XF, s_fa, r_fa)
    fwd_b = exchange(lambda c, k: H.at[c * 2 + k], XP, s_fb, r_fb)
    for m in media:
        m.start()

    def wait_recv(dst, recv, s):
        pltpu.make_async_copy(dst.at[s], dst.at[s], recv.at[s]).wait()

    for f in range(NF):
        for q in range(NQ):
            hi, lo = halves(F[f, q])
            TH[q * SL:(q + 1) * SL, f * LANES:(f + 1) * LANES] = hi
            TL[q * SL:(q + 1) * SL, f * LANES:(f + 1) * LANES] = lo
    for c in small:
        c.wait()
    S[...] = jnp.zeros_like(S)
    lane_r = lanes_of((256, 256))
    lane_l = lanes_of((256, LANES))
    lane8 = lanes_of((256, LANES))

    def gather(i, carry):
        reqs_c = pltpu.make_async_copy(RC.at[i], RC.at[i], r_rc.at[i])
        reqs_w = pltpu.make_async_copy(RW.at[i], RW.at[i], r_rw.at[i])
        reqs_c.wait()
        reqs_w.wait()
        cells = RC[i]
        S[0:4] = (((cells >> 7) & 3) * SL + (cells >> 9)).astype(F32)
        S[4:8] = (cells & 127).astype(F32)
        S[8:12] = RW[i]
        cols = jnp.transpose(S[...])
        icols = cols.astype(jnp.int32)
        for s in range(4):
            hot = lane_r == icols[:, s:s + 1]
            OH[s * 256:(s + 1) * 256] = jnp.where(hot, 1.0, 0.0).astype(BF16)
        masks = [jnp.where(lane_l == icols[:, 4 + s:5 + s], cols[:, 8 + s:9 + s], 0.0) for s in range(4)]
        for s in range(4):
            ACC[s] = masks[s]
        v = jnp.zeros((256, LANES), F32)
        for fp in range(4):
            th = TH[:, fp * 256:(fp + 1) * 256]
            tl = TL[:, fp * 256:(fp + 1) * 256]
            total = None
            for s in range(4):
                hot = OH[s * 256:(s + 1) * 256]
                g = dot(hot, th) + dot(hot, tl)
                w = ACC[s]
                g = g * jnp.concatenate([w, w], axis=1)
                total = g if total is None else total + g
            for h in range(2):
                one = jnp.sum(total[:, h * LANES:(h + 1) * LANES], axis=1, keepdims=True)
                v = jnp.where(lane8 == fp * 2 + h, one, v)
        VS[i] = jnp.transpose(v)[0:8]
        return carry

    def response(i):
        q = (pt + 3 - i) % 4
        return pltpu.make_async_remote_copy(
            src_ref=VS.at[i], dst_ref=VR.at[i], send_sem=s_v.at[i], recv_sem=r_v.at[i],
            device_id={"patch": q}, device_id_type=MESH_ID)

    lax.fori_loop(0, 3, gather, 0)
    for i in range(3):
        response(i).start()

    def tail_of(last_rows, first_rows):
        E[0:MATCH] = last_rows
        E[MATCH:2 * MATCH] = first_rows
        return exact_dot(CM[...], E[0:2 * MATCH])

    for s in range(16):
        wait_recv(XF, r_fa, s)
    for s in range(16):
        hi, lo = halves(XF[s])
        XB[s * SL:(s + 1) * SL, 0:LANES] = hi
        XB[s * SL:(s + 1) * SL, LANES:] = lo
    hi, lo = halves(tail_of(XF[15, SL - MATCH:], XF[0, 0:MATCH]))
    XB[1024:1152, 0:LANES] = hi
    XB[1024:1152, LANES:] = lo

    def rows_a(step, carry):
        i = (zc + step) % 8
        start = pl.multiple_of((7 - i) * LANES, LANES)
        wh = W[0, :, pl.ds(start, P_SIZE)]
        wl = W[1, :, pl.ds(start, P_SIZE)]
        y = dot(wh, XB[...])
        r = y[:, :LANES] + y[:, LANES:] + dot(wl, XB[:, 0:LANES])
        YA[2 * i] = r[0:SL]
        YA[2 * i + 1] = r[SL:]
        return carry

    lax.fori_loop(0, 8, rows_a, 0)
    ret_a = exchange(lambda c, k: YA.at[c * 2 + k], DA, s_ra, r_ra)

    for i in range(3):
        wait_recv(VR, r_v, i)
    S[...] = jnp.zeros_like(S)
    row_r = rows_of((256, 256))
    slot = rows_of((256, LANES))
    for i in range(3):
        q = (pt + i + 1) % 4
        cells = FC[pl.ds(q, 1)]
        S[0:8] = VR[i]
        S[8:9] = (cells & 127).astype(F32)
        cols = jnp.transpose(S[...])
        target = ((cells >> 7) & 3) * SL + (cells >> 9)
        hot = jnp.where(row_r == target, 1.0, 0.0).astype(BF16)
        live = (lane_l == cols[:, 8:9].astype(jnp.int32)) & (slot < cnt[0, 0, 0, q])
        livef = jnp.where(live, 1.0, 0.0)
        part = dot(hot, livef.astype(BF16))
        MK[...] = part if i == 0 else MK[...] + part
        for fp in range(4):
            b = jnp.concatenate([livef * cols[:, 2 * fp:2 * fp + 1], livef * cols[:, 2 * fp + 1:2 * fp + 2]], axis=1)
            hi, lo = halves(b)
            part = dot(hot, hi) + dot(hot, lo)
            SC[fp] = part if i == 0 else SC[fp] + part

    for s in range(16):
        wait_recv(XP, r_fb, s)
    left = lanes_of((SL, LANES)) < 64

    def spread(s):
        x = XP[s]
        r = pltpu.roll(x, 64, 1)
        return jnp.where(left64, x, r), jnp.where(left64, r, x)

    def store_b(at, x):
        hi, lo = halves(x)
        keep = lanes_of(x.shape) < 64
        XB[at:at + x.shape[0], 0:LANES] = jnp.where(keep, hi.astype(F32), lo.astype(F32)).astype(BF16)

    ends = {}
    for s in range(16):
        a, b = spread(s)
        store_b(s * SL, a)
        store_b(s * SL + 32, b)
        if s == 0:
            E[MATCH:2 * MATCH] = a[0:MATCH]
        if s == 15:
            E[0:MATCH] = b[32 - MATCH:]
    store_b(1024, exact_dot(CM[...], E[0:2 * MATCH]))

    def rows_b(step, carry):
        i = (zc + step) % 8
        start = pl.multiple_of((7 - i) * LANES, LANES)
        x = XB[:, 0:LANES]
        y = dot(W[0, :, pl.ds(start, P_SIZE)], x) + dot(W[1, :, pl.ds(start, P_SIZE)], x)
        r = y + pltpu.roll(y, 64, 1)
        YB[2 * i] = jnp.where(left64, r[0:32], r[32:64])
        YB[2 * i + 1] = jnp.where(left64, r[64:96], r[96:128])
        return carry

    lax.fori_loop(0, 8, rows_b, 0)
    ret_b = exchange(lambda c, k: YB.at[c * 2 + k], DB, s_rb, r_rb)

    pltpu.make_async_copy(HN, HN, r_h.at[0]).wait()
    pltpu.make_async_copy(HP, HP, r_h.at[1]).wait()
    for m in media:
        m.wait()
    lane = lanes_of((SL, LANES))
    first = ly == 0
    last = ly == 3
    S[...] = jnp.zeros_like(S)
    S[0:1, 0:64] = PAIR[0].astype(F32)
    S[1:2, 0:64] = PAIR[1].astype(F32)
    pair_cols = jnp.transpose(S[:, 0:LANES]).astype(jnp.int32)
    lane64 = lanes_of((SL, SL))
    pick_el = jnp.where(lane64 == pair_cols[0:64, 0:1], 1.0, 0.0)
    pick_ac = jnp.where(lane64 == pair_cols[0:64, 1:2], 1.0, 0.0)
    pressure = pltpu.roll(exact_dot(pick_el, HP[4]), 1, 1)
    velocity = pltpu.roll(exact_dot(pick_ac, HN[1]), LANES - 1, 1)
    zero_first = jnp.where(first, 0.0, 1.0)
    zero_last = jnp.where(last, 0.0, 1.0)
    one_first = jnp.where(first, 1.0, 0.0)
    one_last = jnp.where(last, 1.0, 0.0)

    for q in range(NQ):
        def dz(f):
            cur = F[f, q]
            prev = F[f, q - 1] if q else HP[f] * zero_first
            nxt = F[f, q + 1] if q < 3 else HN[f] * zero_last
            below = jnp.where(lane == LANES - 1, pltpu.roll(nxt, LANES - 1, 1), pltpu.roll(cur, LANES - 1, 1))
            above = jnp.where(lane == 0, pltpu.roll(prev, 1, 1), pltpu.roll(cur, 1, 1))
            return (below - above) * 0.125

        buoy, lam, mu = MEL[0, q], MEL[1, q], MEL[2, q]
        stiff = lam + 2.0 * mu
        bulk, obuoy = MAC[0, q], MAC[1, q]
        mask = MK[q * SL:(q + 1) * SL] > 0.5

        def put(f, base, coef):
            scat = SC[f // 2, q * SL:(q + 1) * SL, (f % 2) * LANES:(f % 2 + 1) * LANES]
            O[f, q] = jnp.where(mask, scat, base)
            if coef is not None:
                CO[f, q] = jnp.where(mask, 0.0, 0.25 * coef)

        dvz = dz(1)
        put(0, F[0, q] + buoy * dz(3), buoy)
        put(1, F[1, q] + buoy * dz(6), buoy)
        put(2, F[2, q] + lam * dvz, stiff)
        szz = F[6, q] + stiff * dvz
        if q == 0:
            szz = szz + jnp.where(lane == 0, one_first * 0.5 * (-pressure - F[6, q]), 0.0)
        put(6, szz, lam)
        put(3, F[3, q] + mu * dz(0), mu)
        put(4, F[4, q] - bulk * dz(7), -bulk)
        put(5, F[5, q], -obuoy)
        ovz = F[7, q] - obuoy * dz(4)
        if q == 3:
            ovz = ovz + jnp.where(lane == LANES - 1, one_last * 0.5 * (velocity - F[7, q]), 0.0)
        put(7, ovz, None)

    outs = []

    def emit(f, q):
        dst = oel.at[0, EL_OF[f], :, pl.ds(q * LANES, LANES)] if f in EL_OF else oac.at[0, AC_OF[f], :, pl.ds(q * LANES, LANES)]
        c = pltpu.make_async_copy(O.at[f, q], dst, s_out.at[f * NQ + q])
        c.start()
        outs.append(c)

    for q in range(NQ):
        emit(7, q)

    def finish(t, dx):
        f, q = t // 4, t % 4
        for g in FED[f]:
            O[g, q] = O[g, q] + CO[g, q] * dx
            emit(g, q)

    for c in range(8):
        for k in range(2):
            wait_recv(DA, r_ra, 2 * c + k)
            finish(3 * c + 2 * k, DA[2 * c + k])
    for c in range(8):
        wait_recv(DB, r_rb, 2 * c)
        wait_recv(DB, r_rb, 2 * c + 1)
        pa, pb = DB[2 * c], DB[2 * c + 1]
        top = jnp.where(left64, pa, pltpu.roll(pb, 64, 1))
        bot = jnp.where(left64, pltpu.roll(pa, 64, 1), pb)
        finish(3 * c + 1, jnp.concatenate([top, bot], axis=0))

    for r in reqs:
        r.wait_send()
    for i in range(3):
        response(i).wait_send()
    halo_up.wait_send()
    halo_down.wait_send()
    for group in (fwd_a, fwd_b, ret_a, ret_b):
        for r in group:
            r.wait_send()
    for c in outs:
        c.wait()


def per_device(elastic, acoustic, el_media, ac_media, cont_matrix, fringe_cells, donor_cells, donor_weights, donor_counts, el_pair, ac_pair):
    anywhere = pl.BlockSpec(memory_space=pl.ANY)
    vm = pltpu.VMEM
    dma = pltpu.SemaphoreType.DMA
    scratch = [
        vm((NF, NQ, SL, LANES), F32),
        vm((16, 32, LANES), F32),
        vm((16, SL, LANES), F32),
        vm((16, 32, LANES), F32),
        vm((P_SIZE, 256), BF16),
        vm((32, LANES), F32),
        vm((16, SL, LANES), F32),
        vm((16, 32, LANES), F32),
        vm((16, SL, LANES), F32),
        vm((16, 32, LANES), F32),
        vm((2, 128, 2048), BF16),
        vm((128, 2 * MATCH), F32),
        vm((4, 256), jnp.int32),
        vm((2, 1, 64), jnp.int32),
        vm((3, NQ, SL, LANES), F32),
        vm((2, NQ, SL, LANES), F32),
        vm((3, 4, 256), jnp.int32),
        vm((3, 4, 256), F32),
        vm((3, 8, 256), F32),
        vm((3, 8, 256), F32),
        vm((LANES, 256), F32),
        vm((256, 1024), BF16),
        vm((256, 1024), BF16),
        vm((1024, 256), BF16),
        vm((4, 256, LANES), F32),
        vm((4, 256, 256), F32),
        vm((256, LANES), F32),
        vm((NF, SL, LANES), F32),
        vm((NF, SL, LANES), F32),
        vm((NF, NQ, SL, LANES), F32),
        vm((7, NQ, SL, LANES), F32),
        dma((32,)), dma((20,)), dma((5,)),
        dma((15,)), dma((16,)), dma((15,)), dma((16,)),
        dma((15,)), dma((16,)), dma((15,)), dma((16,)),
        dma((3,)), dma((3,)), dma((3,)), dma((3,)), dma((3,)), dma((3,)),
        dma((2,)), dma((2,)), dma((32,)),
    ]
    call = pl.pallas_call(
        kernel,
        out_shape=(jax.ShapeDtypeStruct(elastic.shape, F32), jax.ShapeDtypeStruct(acoustic.shape, F32)),
        in_specs=[pl.BlockSpec(memory_space=pltpu.SMEM)] + [anywhere] * 11,
        out_specs=(anywhere, anywhere),
        scratch_shapes=scratch,
        compiler_params=pltpu.CompilerParams(collective_id=0, has_side_effects=True),
    )
    return call(
        donor_counts, elastic, acoustic, el_media, ac_media, cont_matrix,
        fringe_cells, donor_cells, donor_weights, el_pair, ac_pair, jnp.asarray(derivative_rows()),
    )


def solution(mesh):
    fields = P("patch", None, "line", "layer")
    placed = (
        fields, fields, fields, fields,
        P(),
        P("patch", "line", "layer", None, None),
        P("patch", "line", "layer", None, None, None),
        P("patch", "line", "layer", None, None, None),
        P("patch", "line", "layer", None),
        P("patch", "line"),
        P("patch", "line"),
    )
    return jax.shard_map(per_device, mesh=mesh, in_specs=placed, out_specs=(fields, fields), check_vma=False)
```

profile of v0, /device:TPU:1, one launch (start us, length us, event | category | flops | bytes accessed | tf_op | source)
XLA Modules:
  0.0 53.1 jit_solution(7962648626063449034)
XLA Ops:
  0.6 1.4 %copy.14.cm = f32[128,20]{1,0:T(8,128)} copy(f32[128,20]{0,1:T(8,128)} %param.16) | data formatting | bytes 20480 | tf_op args[4]
  2.1 48.2 %shard_map.131 = (f32[1,5,64,512]{3,2,1,0:T(8,128)}, f32[1,3,64,512]{3,2,1,0:T(8,128)}) custom-call(s32[1,1,1,4]{3,2,1,0:T(1,128)} %cnt.1, f32[1,5,64,512]{3,2,1,0:T(8,128)} %el.1, f32[1,3,64,512]{3,2,1,0:T(8,128)} %ac.1, f32[1,3,64,512]{3,2,1,0:T(8,128)} %em.1, f32[1,2,64,512]{3,2,1,0:T(8,128)} %am.1, f32[128,20]{1,0:T(8,128)} %copy.14.cm, ...), custom_call_target="tpu_custom_call" | custom-call | tf_op jit(solution)/shard_map/pallas_call | solution.py:471
  50.3 0.0 copy-start
  50.3 2.0 %copy.17 = f32[1,5,64,512]{3,2,1,0:T(8,128)} copy(f32[1,5,64,512]{3,2,1,0:T(8,128)} %get-tuple-element.4) | data formatting | bytes 1310720
  52.4 0.0 copy-done
  52.4 0.7 %copy.18 = f32[1,3,64,512]{3,2,1,0:T(8,128)} copy(f32[1,3,64,512]{3,2,1,0:T(8,128)S(1)} %copy-done) | data formatting | bytes 786432
Async XLA Ops:
  50.3 2.1 %copy-start = (f32[1,3,64,512]{3,2,1,0:T(8,128)S(1)}, f32[1,3,64,512]{3,2,1,0:T(8,128)}, u32[]{:S(2)}) copy-start(f32[1,3,64,512]{3,2,1,0:T(8,128)} %get-tuple-element.5) | copy-start | bytes 1179652
where the time goes:
time: 53.3 us; the launch traced here: 53.1 us
  Pallas kernels  48.2 us (90%)
  local copies, waits for them, and re-layouts  4.23 us (8%)
  between operations  0.65 us (1%)
    pallas_call x1, Pallas kernels, per_device(): call(donor_counts, elastic, acoustic, el_media, ac_media, cont_matrix, fr...  48.2 us
    unnamed x5, local copies, waits for them, and re-layouts  4.23 us

commit v1 on v0

--- a/solution.py
+++ b/solution.py
@@ -59,10 +59,10 @@
 def kernel(
     cnt, el, ac, em, am, cm, fc, dc, dw, elp, acp, wt,
     oel, oac,
-    F, H, XF, XP, XB, E, YA, YB, DA, DB, W, CM, FC, PAIR, MEL, MAC,
-    RC, RW, VS, VR, S, TH, TL, OH, ACC, SC, MK, HP, HN, O, CO,
+    F, H, XF, XP, XB, E, YA, YB, DA, DB, W, CM, C128, FC, PAIR, MEL, MAC,
+    RC, RW, VS, VR, S, TH, TL, OH, ACC, SC, MK, HP, HN, CO,
     s_load, s_med, s_small, s_fa, r_fa, s_fb, r_fb, s_ra, r_ra, s_rb, r_rb,
-    s_rc, r_rc, s_rw, r_rw, s_v, r_v, s_h, r_h, s_out,
+    s_rc, r_rc, s_rw, r_rw, s_v, r_v, s_h, r_h,
 ):
     me = lax.axis_index("line")
     zc = me // 2
@@ -72,6 +72,17 @@
 
     def line_of(dz, k):
         return ((zc + dz + 8) % 8) * 2 + k
+
+    def out_of(f, q):
+        cols = slice(q * LANES, (q + 1) * LANES)
+        return (oel, (0, EL_OF[f], slice(None), cols)) if f in EL_OF else (oac, (0, AC_OF[f], slice(None), cols))
+
+    barrier = pltpu.get_barrier_semaphore()
+    partners = [{"line": (me + o) % 16} for o in range(1, 16)]
+    partners += [{"patch": (pt + o) % 4} for o in range(1, 4)]
+    partners += [{"layer": (ly + o) % 4} for o in (1, 3)]
+    for p in partners:
+        pl.semaphore_signal(barrier, inc=1, device_id=p, device_id_type=MESH_ID)
 
     loads = {}
     for f in range(NF):
@@ -96,23 +107,9 @@
         for q in range(NQ):
             media.append(pltpu.make_async_copy(am.at[0, f, :, pl.ds(q * LANES, LANES)], MAC.at[f, q], s_med.at[12 + f * NQ + q]))
 
-    barrier = pltpu.get_barrier_semaphore()
-    partners = [{"line": (me + o) % 16} for o in range(1, 16)]
-    partners += [{"patch": (pt + o) % 4} for o in range(1, 4)]
-    partners += [{"layer": (ly + o) % 4} for o in (1, 3)]
-    for p in partners:
-        pl.semaphore_signal(barrier, inc=1, device_id=p, device_id_type=MESH_ID)
-
     for f in range(6):
         for q in range(NQ):
             loads[f, q].wait()
-    left64 = lanes_of((32, LANES)) < 64
-    for c in range(8):
-        t = 3 * c + 1
-        top = F[t // 4, t % 4, 0:32]
-        bot = F[t // 4, t % 4, 32:64]
-        H[2 * c] = jnp.where(left64, top, pltpu.roll(bot, 64, 1))
-        H[2 * c + 1] = jnp.where(left64, pltpu.roll(top, 64, 1), bot)
     for f in range(6, 8):
         for q in range(NQ):
             loads[f, q].wait()
@@ -145,8 +142,7 @@
 
     def targets():
         for i, (dz, k) in enumerate(order):
-            kk = k if i % 2 == k else k
-            yield i, (zc + dz + 8) % 8, kk
+            yield i, (zc + dz + 8) % 8, k
         yield n_out, zc, other
 
     def exchange(src_of, dst, send, recv):
@@ -166,7 +162,13 @@
         return F.at[t // 4, t % 4]
 
     fwd_a = exchange(full_tile, XF, s_fa, r_fa)
-    fwd_b = exchange(lambda c, k: H.at[c * 2 + k], XP, s_fb, r_fb)
+    left64 = lanes_of((32, LANES)) < 64
+    for c in range(8):
+        t = 3 * c + 1
+        top = F[t // 4, t % 4, 0:32]
+        bot = F[t // 4, t % 4, 32:64]
+        H[2 * c] = jnp.where(left64, top, pltpu.roll(bot, 64, 1))
+        H[2 * c + 1] = jnp.where(left64, pltpu.roll(top, 64, 1), bot)
     for m in media:
         m.start()
 
@@ -178,8 +180,13 @@
             hi, lo = halves(F[f, q])
             TH[q * SL:(q + 1) * SL, f * LANES:(f + 1) * LANES] = hi
             TL[q * SL:(q + 1) * SL, f * LANES:(f + 1) * LANES] = lo
+    fwd_b = exchange(lambda c, k: H.at[c * 2 + k], XP, s_fb, r_fb)
     for c in small:
         c.wait()
+    S[...] = jnp.zeros_like(S)
+    S[0:2 * MATCH] = jnp.concatenate([CM[...], CM[...]], axis=1)
+    C128[...] = jnp.transpose(S[...])[0:LANES]
+    E[...] = jnp.zeros_like(E)
     S[...] = jnp.zeros_like(S)
     lane_r = lanes_of((256, 256))
     lane_l = lanes_of((256, LANES))
@@ -229,23 +236,45 @@
     for i in range(3):
         response(i).start()
 
-    def tail_of(last_rows, first_rows):
-        E[0:MATCH] = last_rows
-        E[MATCH:2 * MATCH] = first_rows
-        return exact_dot(CM[...], E[0:2 * MATCH])
-
-    for s in range(16):
+    def far_first(step):
+        return ((8 - step) // 2) * (2 * (step % 2) - 1)
+
+    arrivals = [(zc, core), (zc, other)] + [((zc + dz + 8) % 8, k) for dz in (1, -1, 2, -2, 3, -3, 4) for k in (0, 1)]
+
+    def send_block(step, src, dst, send, recv):
+        c = (zc + far_first(step) + 8) % 8
+        for k in range(2):
+            pltpu.make_async_remote_copy(
+                src_ref=src.at[2 * c + k], dst_ref=dst.at[me], send_sem=send.at[2 * step + k], recv_sem=recv.at[me],
+                device_id={"line": 2 * c + k}, device_id_type=MESH_ID).start()
+
+    def send_last(src, dst, send, recv):
+        pltpu.make_async_remote_copy(
+            src_ref=src.at[2 * zc + other], dst_ref=dst.at[me], send_sem=send.at[14], recv_sem=recv.at[me],
+            device_id={"line": 2 * zc + other}, device_id_type=MESH_ID).start()
+        pltpu.make_async_copy(src.at[me], dst.at[me], recv.at[me]).start()
+
+    def wait_sent(src, dst, send, recv):
+        for i in range(15):
+            pltpu.make_async_remote_copy(
+                src_ref=src.at[0], dst_ref=dst.at[0], send_sem=send.at[i], recv_sem=recv.at[0],
+                device_id={"line": 2 * zc + other}, device_id_type=MESH_ID).wait_send()
+
+    def store_a(at, x):
+        hi, lo = halves(x)
+        XB[pl.ds(at, x.shape[0]), 0:LANES] = hi
+        XB[pl.ds(at, x.shape[0]), LANES:] = lo
+
+    for c, k in arrivals:
+        s = 2 * c + k
         wait_recv(XF, r_fa, s)
-    for s in range(16):
-        hi, lo = halves(XF[s])
-        XB[s * SL:(s + 1) * SL, 0:LANES] = hi
-        XB[s * SL:(s + 1) * SL, LANES:] = lo
-    hi, lo = halves(tail_of(XF[15, SL - MATCH:], XF[0, 0:MATCH]))
-    XB[1024:1152, 0:LANES] = hi
-    XB[1024:1152, LANES:] = lo
+        store_a(pl.multiple_of(s * SL, SL), XF[s])
+    E[0:MATCH] = XF[15, SL - MATCH:]
+    E[MATCH:2 * MATCH] = XF[0, 0:MATCH]
+    store_a(1024, exact_dot(C128[...], E[...]))
 
     def rows_a(step, carry):
-        i = (zc + step) % 8
+        i = (zc + far_first(step) + 8) % 8
         start = pl.multiple_of((7 - i) * LANES, LANES)
         wh = W[0, :, pl.ds(start, P_SIZE)]
         wl = W[1, :, pl.ds(start, P_SIZE)]
@@ -253,10 +282,15 @@
         r = y[:, :LANES] + y[:, LANES:] + dot(wl, XB[:, 0:LANES])
         YA[2 * i] = r[0:SL]
         YA[2 * i + 1] = r[SL:]
+
+        @pl.when(step > 0)
+        def _():
+            send_block(step - 1, YA, DA, s_ra, r_ra)
+
         return carry
 
     lax.fori_loop(0, 8, rows_a, 0)
-    ret_a = exchange(lambda c, k: YA.at[c * 2 + k], DA, s_ra, r_ra)
+    send_last(YA, DA, s_ra, r_ra)
 
     for i in range(3):
         wait_recv(VR, r_v, i)
@@ -281,43 +315,42 @@
             part = dot(hot, hi) + dot(hot, lo)
             SC[fp] = part if i == 0 else SC[fp] + part
 
-    for s in range(16):
-        wait_recv(XP, r_fb, s)
-    left = lanes_of((SL, LANES)) < 64
-
-    def spread(s):
-        x = XP[s]
+    def spread(x):
         r = pltpu.roll(x, 64, 1)
         return jnp.where(left64, x, r), jnp.where(left64, r, x)
 
     def store_b(at, x):
         hi, lo = halves(x)
         keep = lanes_of(x.shape) < 64
-        XB[at:at + x.shape[0], 0:LANES] = jnp.where(keep, hi.astype(F32), lo.astype(F32)).astype(BF16)
-
-    ends = {}
-    for s in range(16):
-        a, b = spread(s)
-        store_b(s * SL, a)
-        store_b(s * SL + 32, b)
-        if s == 0:
-            E[MATCH:2 * MATCH] = a[0:MATCH]
-        if s == 15:
-            E[0:MATCH] = b[32 - MATCH:]
-    store_b(1024, exact_dot(CM[...], E[0:2 * MATCH]))
+        XB[pl.ds(at, x.shape[0]), 0:LANES] = jnp.where(keep, hi.astype(F32), lo.astype(F32)).astype(BF16)
+
+    for c, k in arrivals:
+        s = 2 * c + k
+        wait_recv(XP, r_fb, s)
+        a, b = spread(XP[s])
+        store_b(pl.multiple_of(s * SL, SL), a)
+        store_b(pl.multiple_of(s * SL + 32, 32), b)
+    E[0:MATCH] = spread(XP[15])[1][32 - MATCH:]
+    E[MATCH:2 * MATCH] = spread(XP[0])[0][0:MATCH]
+    store_b(1024, exact_dot(C128[...], E[...]))
 
     def rows_b(step, carry):
-        i = (zc + step) % 8
+        i = (zc + far_first(step) + 8) % 8
         start = pl.multiple_of((7 - i) * LANES, LANES)
         x = XB[:, 0:LANES]
         y = dot(W[0, :, pl.ds(start, P_SIZE)], x) + dot(W[1, :, pl.ds(start, P_SIZE)], x)
         r = y + pltpu.roll(y, 64, 1)
         YB[2 * i] = jnp.where(left64, r[0:32], r[32:64])
         YB[2 * i + 1] = jnp.where(left64, r[64:96], r[96:128])
+
+        @pl.when(step > 0)
+        def _():
+            send_block(step - 1, YB, DB, s_rb, r_rb)
+
         return carry
 
     lax.fori_loop(0, 8, rows_b, 0)
-    ret_b = exchange(lambda c, k: YB.at[c * 2 + k], DB, s_rb, r_rb)
+    send_last(YB, DB, s_rb, r_rb)
 
     pltpu.make_async_copy(HN, HN, r_h.at[0]).wait()
     pltpu.make_async_copy(HP, HP, r_h.at[1]).wait()
@@ -356,7 +389,8 @@
 
         def put(f, base, coef):
             scat = SC[f // 2, q * SL:(q + 1) * SL, (f % 2) * LANES:(f % 2 + 1) * LANES]
-            O[f, q] = jnp.where(mask, scat, base)
+            ref, at = out_of(f, q)
+            ref[at] = jnp.where(mask, scat, base)
             if coef is not None:
                 CO[f, q] = jnp.where(mask, 0.0, 0.25 * coef)
 
@@ -376,22 +410,11 @@
             ovz = ovz + jnp.where(lane == LANES - 1, one_last * 0.5 * (velocity - F[7, q]), 0.0)
         put(7, ovz, None)
 
-    outs = []
-
-    def emit(f, q):
-        dst = oel.at[0, EL_OF[f], :, pl.ds(q * LANES, LANES)] if f in EL_OF else oac.at[0, AC_OF[f], :, pl.ds(q * LANES, LANES)]
-        c = pltpu.make_async_copy(O.at[f, q], dst, s_out.at[f * NQ + q])
-        c.start()
-        outs.append(c)
-
-    for q in range(NQ):
-        emit(7, q)
-
     def finish(t, dx):
         f, q = t // 4, t % 4
         for g in FED[f]:
-            O[g, q] = O[g, q] + CO[g, q] * dx
-            emit(g, q)
+            ref, at = out_of(g, q)
+            ref[at] = ref[at] + CO[g, q] * dx
 
     for c in range(8):
         for k in range(2):
@@ -411,11 +434,11 @@
         response(i).wait_send()
     halo_up.wait_send()
     halo_down.wait_send()
-    for group in (fwd_a, fwd_b, ret_a, ret_b):
+    for group in (fwd_a, fwd_b):
         for r in group:
             r.wait_send()
-    for c in outs:
-        c.wait()
+    wait_sent(YA, DA, s_ra, r_ra)
+    wait_sent(YB, DB, s_rb, r_rb)
 
 
 def per_device(elastic, acoustic, el_media, ac_media, cont_matrix, fringe_cells, donor_cells, donor_weights, donor_counts, el_pair, ac_pair):
@@ -428,13 +451,14 @@
         vm((16, SL, LANES), F32),
         vm((16, 32, LANES), F32),
         vm((P_SIZE, 256), BF16),
-        vm((32, LANES), F32),
+        vm((LANES, LANES), F32),
         vm((16, SL, LANES), F32),
         vm((16, 32, LANES), F32),
         vm((16, SL, LANES), F32),
         vm((16, 32, LANES), F32),
         vm((2, 128, 2048), BF16),
-        vm((128, 2 * MATCH), F32),
+        vm((2 * MATCH, 128), F32),
+        vm((LANES, LANES), F32),
         vm((4, 256), jnp.int32),
         vm((2, 1, 64), jnp.int32),
         vm((3, NQ, SL, LANES), F32),
@@ -452,24 +476,23 @@
         vm((256, LANES), F32),
         vm((NF, SL, LANES), F32),
         vm((NF, SL, LANES), F32),
-        vm((NF, NQ, SL, LANES), F32),
         vm((7, NQ, SL, LANES), F32),
         dma((32,)), dma((20,)), dma((5,)),
         dma((15,)), dma((16,)), dma((15,)), dma((16,)),
         dma((15,)), dma((16,)), dma((15,)), dma((16,)),
         dma((3,)), dma((3,)), dma((3,)), dma((3,)), dma((3,)), dma((3,)),
-        dma((2,)), dma((2,)), dma((32,)),
+        dma((2,)), dma((2,)),
     ]
     call = pl.pallas_call(
         kernel,
-        out_shape=(jax.ShapeDtypeStruct(elastic.shape, F32), jax.ShapeDtypeStruct(acoustic.shape, F32)),
+        out_shape=(pltpu.VMEM(elastic.shape, F32), pltpu.VMEM(acoustic.shape, F32)),
         in_specs=[pl.BlockSpec(memory_space=pltpu.SMEM)] + [anywhere] * 11,
-        out_specs=(anywhere, anywhere),
+        out_specs=(pl.BlockSpec(memory_space=pltpu.VMEM),) * 2,
         scratch_shapes=scratch,
         compiler_params=pltpu.CompilerParams(collective_id=0, has_side_effects=True),
     )
     return call(
-        donor_counts, elastic, acoustic, el_media, ac_media, cont_matrix,
+        donor_counts, elastic, acoustic, el_media, ac_media, cont_matrix.T,
         fringe_cells, donor_cells, donor_weights, el_pair, ac_pair, jnp.asarray(derivative_rows()),
     )
 

time: 53.3 us -> 49.8 us (0.934)
  local copies, waits for them, and re-layouts: 4.23 us -> 1.58 us
  Pallas kernels: 48.2 us -> 47.5 us
    unnamed x5 -> x2, local copies, waits for them, and re-layouts: 4.23 us -> 1.58 us
    pallas_call x1, Pallas kernels: 48.2 us -> 47.5 us  [per_device(): call(donor_counts, elastic, acoustic, el_media, ac_media, cont_matrix.T,...]
where the time goes in v1:
time: 49.8 us; the launch traced here: 49.7 us
  Pallas kernels  47.5 us (95%)
  local copies, waits for them, and re-layouts  1.58 us (3%)
  between operations  0.64 us (1%)
    pallas_call x1, Pallas kernels, per_device(): call(donor_counts, elastic, acoustic, el_media, ac_media, cont_matrix.T,...  47.5 us
    unnamed x2, local copies, waits for them, and re-layouts  1.58 us

profile of v1, /device:TPU:1, one launch (start us, length us, event | category | flops | bytes accessed | tf_op | source)
XLA Modules:
  0.0 49.7 jit_solution(1093603760571252480)
XLA Ops:
  0.6 47.5 %shard_map.131 = (f32[1,5,64,512]{3,2,1,0:T(8,128)S(1)}, f32[1,3,64,512]{3,2,1,0:T(8,128)S(1)}) custom-call(s32[1,1,1,4]{3,2,1,0:T(1,128)} %cnt.1, f32[1,5,64,512]{3,2,1,0:T(8,128)} %el.1, f32[1,3,64,512]{3,2,1,0:T(8,128)} %ac.1, f32[1,3,64,512]{3,2,1,0:T(8,128)} %em.1, f32[1,2,64,512]{3,2,1,0:T(8,128)} %am.1, f32[20,128]{1,0:T(8,128)} %bitcast.1, ...), custom_call_target="tpu_custom_call" | custom-call | tf_op jit(solution)/shard_map/pallas_call | solution.py:494
  48.1 0.8 %copy.16 = f32[1,5,64,512]{3,2,1,0:T(8,128)} copy(f32[1,5,64,512]{3,2,1,0:T(8,128)S(1)} %get-tuple-element.2) | data formatting | bytes 1310720
  48.9 0.7 %copy.17 = f32[1,3,64,512]{3,2,1,0:T(8,128)} copy(f32[1,3,64,512]{3,2,1,0:T(8,128)S(1)} %get-tuple-element.3) | data formatting | bytes 786432

commit v2 on v1

--- a/solution.py
+++ b/solution.py
@@ -56,11 +56,43 @@
     return lax.broadcasted_iota(jnp.int32, shape, len(shape) - 2)
 
 
+def tile_of(oel, oac, f, q):
+    cols = pl.ds(q * LANES, LANES)
+    return oel.at[0, EL_OF[f], :, cols] if f in EL_OF else oac.at[0, AC_OF[f], :, cols]
+
+
+def finish(bel, bac, CO, DA, DB, oel, oac, O, sem):
+    left64 = lanes_of((32, LANES)) < 64
+    outs = []
+
+    def emit(f, q, value):
+        O[f, q] = value
+        outs.append(pltpu.make_async_copy(O.at[f, q], tile_of(oel, oac, f, q), sem.at[f * NQ + q]))
+        outs[-1].start()
+
+    for q in range(NQ):
+        emit(7, q, tile_of(bel, bac, 7, q)[...])
+    for t in range(24):
+        c, part = t // 3, t % 3
+        if part == 1:
+            pa, pb = DB[2 * c], DB[2 * c + 1]
+            top = jnp.where(left64, pa, pltpu.roll(pb, 64, 1))
+            bot = jnp.where(left64, pltpu.roll(pa, 64, 1), pb)
+            dx = jnp.concatenate([top, bot], axis=0)
+        else:
+            dx = DA[2 * c + part // 2]
+        f, q = t // 4, t % 4
+        for g in FED[f]:
+            emit(g, q, tile_of(bel, bac, g, q)[...] + CO[g, q] * dx)
+    for c in outs:
+        c.wait()
+
+
 def kernel(
     cnt, el, ac, em, am, cm, fc, dc, dw, elp, acp, wt,
-    oel, oac,
-    F, H, XF, XP, XB, E, YA, YB, DA, DB, W, CM, C128, FC, PAIR, MEL, MAC,
-    RC, RW, VS, VR, S, TH, TL, OH, ACC, SC, MK, HP, HN, CO,
+    oel, oac, CO, DA, DB,
+    F, H, XF, XP, XB, E, YA, YB, W, CM, C128, FC, PAIR, CNT, MEL, MAC,
+    RC, RW, VS, VR, S, TH, TL, OH, ACC, SC, MK, HP, HN,
     s_load, s_med, s_small, s_fa, r_fa, s_fb, r_fb, s_ra, r_ra, s_rb, r_rb,
     s_rc, r_rc, s_rw, r_rw, s_v, r_v, s_h, r_h,
 ):
@@ -72,10 +104,6 @@
 
     def line_of(dz, k):
         return ((zc + dz + 8) % 8) * 2 + k
-
-    def out_of(f, q):
-        cols = slice(q * LANES, (q + 1) * LANES)
-        return (oel, (0, EL_OF[f], slice(None), cols)) if f in EL_OF else (oac, (0, AC_OF[f], slice(None), cols))
 
     barrier = pltpu.get_barrier_semaphore()
     partners = [{"line": (me + o) % 16} for o in range(1, 16)]
@@ -96,6 +124,7 @@
         pltpu.make_async_copy(fc.at[0, 0, 0], FC, s_small.at[2]),
         pltpu.make_async_copy(elp, PAIR.at[0], s_small.at[3]),
         pltpu.make_async_copy(acp, PAIR.at[1], s_small.at[4]),
+        pltpu.make_async_copy(cnt, CNT, s_small.at[5]),
     ]
     for c in small:
         c.start()
@@ -305,7 +334,7 @@
         cols = jnp.transpose(S[...])
         target = ((cells >> 7) & 3) * SL + (cells >> 9)
         hot = jnp.where(row_r == target, 1.0, 0.0).astype(BF16)
-        live = (lane_l == cols[:, 8:9].astype(jnp.int32)) & (slot < cnt[0, 0, 0, q])
+        live = (lane_l == cols[:, 8:9].astype(jnp.int32)) & (slot < CNT[0, 0, 0, q])
         livef = jnp.where(live, 1.0, 0.0)
         part = dot(hot, livef.astype(BF16))
         MK[...] = part if i == 0 else MK[...] + part
@@ -389,8 +418,7 @@
 
         def put(f, base, coef):
             scat = SC[f // 2, q * SL:(q + 1) * SL, (f % 2) * LANES:(f % 2 + 1) * LANES]
-            ref, at = out_of(f, q)
-            ref[at] = jnp.where(mask, scat, base)
+            tile_of(oel, oac, f, q)[...] = jnp.where(mask, scat, base)
             if coef is not None:
                 CO[f, q] = jnp.where(mask, 0.0, 0.25 * coef)
 
@@ -410,23 +438,10 @@
             ovz = ovz + jnp.where(lane == LANES - 1, one_last * 0.5 * (velocity - F[7, q]), 0.0)
         put(7, ovz, None)
 
-    def finish(t, dx):
-        f, q = t // 4, t % 4
-        for g in FED[f]:
-            ref, at = out_of(g, q)
-            ref[at] = ref[at] + CO[g, q] * dx
-
-    for c in range(8):
-        for k in range(2):
-            wait_recv(DA, r_ra, 2 * c + k)
-            finish(3 * c + 2 * k, DA[2 * c + k])
-    for c in range(8):
-        wait_recv(DB, r_rb, 2 * c)
-        wait_recv(DB, r_rb, 2 * c + 1)
-        pa, pb = DB[2 * c], DB[2 * c + 1]
-        top = jnp.where(left64, pa, pltpu.roll(pb, 64, 1))
-        bot = jnp.where(left64, pltpu.roll(pa, 64, 1), pb)
-        finish(3 * c + 1, jnp.concatenate([top, bot], axis=0))
+    for i in range(16):
+        wait_recv(DA, r_ra, i)
+    for i in range(16):
+        wait_recv(DB, r_rb, i)
 
     for r in reqs:
         r.wait_send()
@@ -454,13 +469,12 @@
         vm((LANES, LANES), F32),
         vm((16, SL, LANES), F32),
         vm((16, 32, LANES), F32),
-        vm((16, SL, LANES), F32),
-        vm((16, 32, LANES), F32),
         vm((2, 128, 2048), BF16),
         vm((2 * MATCH, 128), F32),
         vm((LANES, LANES), F32),
         vm((4, 256), jnp.int32),
         vm((2, 1, 64), jnp.int32),
+        pltpu.SMEM((1, 1, 1, 4), jnp.int32),
         vm((3, NQ, SL, LANES), F32),
         vm((2, NQ, SL, LANES), F32),
         vm((3, 4, 256), jnp.int32),
@@ -476,8 +490,7 @@
         vm((256, LANES), F32),
         vm((NF, SL, LANES), F32),
         vm((NF, SL, LANES), F32),
-        vm((7, NQ, SL, LANES), F32),
-        dma((32,)), dma((20,)), dma((5,)),
+        dma((32,)), dma((20,)), dma((6,)),
         dma((15,)), dma((16,)), dma((15,)), dma((16,)),
         dma((15,)), dma((16,)), dma((15,)), dma((16,)),
         dma((3,)), dma((3,)), dma((3,)), dma((3,)), dma((3,)), dma((3,)),
@@ -485,16 +498,27 @@
     ]
     call = pl.pallas_call(
         kernel,
-        out_shape=(pltpu.VMEM(elastic.shape, F32), pltpu.VMEM(acoustic.shape, F32)),
-        in_specs=[pl.BlockSpec(memory_space=pltpu.SMEM)] + [anywhere] * 11,
-        out_specs=(pl.BlockSpec(memory_space=pltpu.VMEM),) * 2,
+        out_shape=(
+            vm(elastic.shape, F32), vm(acoustic.shape, F32), vm((7, NQ, SL, LANES), F32),
+            vm((16, SL, LANES), F32), vm((16, 32, LANES), F32),
+        ),
+        in_specs=[anywhere] * 12,
+        out_specs=(pl.BlockSpec(memory_space=pltpu.VMEM),) * 5,
         scratch_shapes=scratch,
         compiler_params=pltpu.CompilerParams(collective_id=0, has_side_effects=True),
     )
-    return call(
+    parts = call(
         donor_counts, elastic, acoustic, el_media, ac_media, cont_matrix.T,
         fringe_cells, donor_cells, donor_weights, el_pair, ac_pair, jnp.asarray(derivative_rows()),
     )
+    return pl.pallas_call(
+        finish,
+        out_shape=(jax.ShapeDtypeStruct(elastic.shape, F32), jax.ShapeDtypeStruct(acoustic.shape, F32)),
+        in_specs=[pl.BlockSpec(memory_space=pltpu.VMEM)] * 5,
+        out_specs=(anywhere, anywhere),
+        scratch_shapes=[vm((NF, NQ, SL, LANES), F32), dma((32,))],
+        compiler_params=pltpu.CompilerParams(vmem_limit_bytes=16 * 2**20),
+    )(*parts)
 
 
 def solution(mesh):

time: 49.8 us -> 48.3 us (0.970)
  local copies, waits for them, and re-layouts: 1.58 us -> 0 us
    unnamed x2 -> x0, local copies, waits for them, and re-layouts: 1.58 us -> none
    pallas_call x0 -> x1, Pallas kernels: none -> 1.25 us  [per_device(): pl.pallas_call(finish, out_shape=(jax.ShapeDtypeStruct(elastic.shape, F32...]
    pallas_call x1, Pallas kernels: 47.5 us -> 46.3 us  [per_device(): call(donor_counts, elastic, acoustic, el_media, ac_media, cont_matrix.T,...]
where the time goes in v2:
time: 48.3 us; the launch traced here: 48.2 us
  Pallas kernels  47.5 us (98%)
  between operations  0.64 us (1%)
    pallas_call x1, Pallas kernels, per_device(): call(donor_counts, elastic, acoustic, el_media, ac_media, cont_matrix.T,...  46.3 us
    pallas_call x1, Pallas kernels, per_device(): pl.pallas_call(finish, out_shape=(jax.ShapeDtypeStruct(elastic.shape, F32...  1.25 us

profile of v2, /device:TPU:1, one launch (start us, length us, event | category | flops | bytes accessed | tf_op | source)
XLA Modules:
  0.0 48.2 jit_solution(1690722969670367371)
XLA Ops:
  0.6 46.3 %shard_map.131 = (f32[1,5,64,512]{3,2,1,0:T(8,128)S(1)}, f32[1,3,64,512]{3,2,1,0:T(8,128)S(1)}, f32[7,4,64,128]{3,2,1,0:T(8,128)S(1)}, f32[16,64,128]{2,1,0:T(8,128)S(1)}, f32[16,32,128]{2,1,0:T(8,128)S(1)}) custom-call(s32[1,1,1,4]{3,2,1,0:T(1,128)} %cnt.1, f32[1,5,64,512]{3,2,1,0:T(8,128)} %el.1, f32[1,3,64,512]{3,2,1,0:T(8,128)} %ac.1, ...), custom_call_target="tpu_custom_call" | custom-call | tf_op jit(solution)/shard_map/pallas_call | solution.py:510
  46.9 1.2 %shard_map.132 = (f32[1,5,64,512]{3,2,1,0:T(8,128)}, f32[1,3,64,512]{3,2,1,0:T(8,128)}) custom-call(f32[1,5,64,512]{3,2,1,0:T(8,128)S(1)} %get-tuple-element.7.bel, f32[1,3,64,512]{3,2,1,0:T(8,128)S(1)} %get-tuple-element.8.bac, f32[7,4,64,128]{3,2,1,0:T(8,128)S(1)} %get-tuple-element.9.CO, f32[16,64,128]{2,1,0:T(8,128)S(1)} %get-tuple-element.10.DA, ...), custom_call_target="tpu_custom_call" | custom-call | tf_op jit(solution)/shard_map/pallas_call | solution.py:514

commit v3 on v2

--- a/solution.py
+++ b/solution.py
@@ -139,6 +139,13 @@
     for f in range(6):
         for q in range(NQ):
             loads[f, q].wait()
+    left64 = lanes_of((32, LANES)) < 64
+    for c in range(8):
+        t = 3 * c + 1
+        top = F[t // 4, t % 4, 0:32]
+        bot = F[t // 4, t % 4, 32:64]
+        H[2 * c] = jnp.where(left64, top, pltpu.roll(bot, 64, 1))
+        H[2 * c + 1] = jnp.where(left64, pltpu.roll(top, 64, 1), bot)
     for f in range(6, 8):
         for q in range(NQ):
             loads[f, q].wait()
@@ -190,14 +197,8 @@
         t = 3 * c + 2 * k
         return F.at[t // 4, t % 4]
 
+    fwd_b = exchange(lambda c, k: H.at[c * 2 + k], XP, s_fb, r_fb)
     fwd_a = exchange(full_tile, XF, s_fa, r_fa)
-    left64 = lanes_of((32, LANES)) < 64
-    for c in range(8):
-        t = 3 * c + 1
-        top = F[t // 4, t % 4, 0:32]
-        bot = F[t // 4, t % 4, 32:64]
-        H[2 * c] = jnp.where(left64, top, pltpu.roll(bot, 64, 1))
-        H[2 * c + 1] = jnp.where(left64, pltpu.roll(top, 64, 1), bot)
     for m in media:
         m.start()
 
@@ -209,7 +210,6 @@
             hi, lo = halves(F[f, q])
             TH[q * SL:(q + 1) * SL, f * LANES:(f + 1) * LANES] = hi
             TL[q * SL:(q + 1) * SL, f * LANES:(f + 1) * LANES] = lo
-    fwd_b = exchange(lambda c, k: H.at[c * 2 + k], XP, s_fb, r_fb)
     for c in small:
         c.wait()
     S[...] = jnp.zeros_like(S)
@@ -265,61 +265,70 @@
     for i in range(3):
         response(i).start()
 
-    def far_first(step):
-        return ((8 - step) // 2) * (2 * (step % 2) - 1)
-
     arrivals = [(zc, core), (zc, other)] + [((zc + dz + 8) % 8, k) for dz in (1, -1, 2, -2, 3, -3, 4) for k in (0, 1)]
 
-    def send_block(step, src, dst, send, recv):
-        c = (zc + far_first(step) + 8) % 8
+    def send_block(i, src, dst, send, recv):
         for k in range(2):
-            pltpu.make_async_remote_copy(
-                src_ref=src.at[2 * c + k], dst_ref=dst.at[me], send_sem=send.at[2 * step + k], recv_sem=recv.at[me],
-                device_id={"line": 2 * c + k}, device_id_type=MESH_ID).start()
-
-    def send_last(src, dst, send, recv):
-        pltpu.make_async_remote_copy(
-            src_ref=src.at[2 * zc + other], dst_ref=dst.at[me], send_sem=send.at[14], recv_sem=recv.at[me],
-            device_id={"line": 2 * zc + other}, device_id_type=MESH_ID).start()
-        pltpu.make_async_copy(src.at[me], dst.at[me], recv.at[me]).start()
+            t = 2 * i + k
+
+            @pl.when(t != me)
+            def _():
+                pltpu.make_async_remote_copy(
+                    src_ref=src.at[t], dst_ref=dst.at[me], send_sem=send.at[t], recv_sem=recv.at[me],
+                    device_id={"line": t}, device_id_type=MESH_ID).start()
+
+            @pl.when(t == me)
+            def _():
+                pltpu.make_async_copy(src.at[me], dst.at[me], recv.at[me]).start()
 
     def wait_sent(src, dst, send, recv):
-        for i in range(15):
-            pltpu.make_async_remote_copy(
-                src_ref=src.at[0], dst_ref=dst.at[0], send_sem=send.at[i], recv_sem=recv.at[0],
-                device_id={"line": 2 * zc + other}, device_id_type=MESH_ID).wait_send()
+        for t in range(16):
+            @pl.when(t != me)
+            def _():
+                pltpu.make_async_remote_copy(
+                    src_ref=src.at[t], dst_ref=dst.at[me], send_sem=send.at[t], recv_sem=recv.at[me],
+                    device_id={"line": t}, device_id_type=MESH_ID).wait_send()
 
     def store_a(at, x):
         hi, lo = halves(x)
         XB[pl.ds(at, x.shape[0]), 0:LANES] = hi
         XB[pl.ds(at, x.shape[0]), LANES:] = lo
 
+    def spread(x):
+        r = pltpu.roll(x, 64, 1)
+        return jnp.where(left64, x, r), jnp.where(left64, r, x)
+
+    def store_b(at, x):
+        hi, lo = halves(x)
+        keep = lanes_of(x.shape) < 64
+        XB[pl.ds(at, x.shape[0]), 0:LANES] = jnp.where(keep, hi.astype(F32), lo.astype(F32)).astype(BF16)
+
     for c, k in arrivals:
         s = 2 * c + k
-        wait_recv(XF, r_fa, s)
-        store_a(pl.multiple_of(s * SL, SL), XF[s])
-    E[0:MATCH] = XF[15, SL - MATCH:]
-    E[MATCH:2 * MATCH] = XF[0, 0:MATCH]
-    store_a(1024, exact_dot(C128[...], E[...]))
-
-    def rows_a(step, carry):
-        i = (zc + far_first(step) + 8) % 8
+        wait_recv(XP, r_fb, s)
+        a, b = spread(XP[s])
+        store_b(pl.multiple_of(s * SL, SL), a)
+        store_b(pl.multiple_of(s * SL + 32, 32), b)
+    E[0:MATCH] = spread(XP[15])[1][32 - MATCH:]
+    E[MATCH:2 * MATCH] = spread(XP[0])[0][0:MATCH]
+    store_b(1024, exact_dot(C128[...], E[...]))
+
+    def rows_b(i, carry):
         start = pl.multiple_of((7 - i) * LANES, LANES)
-        wh = W[0, :, pl.ds(start, P_SIZE)]
-        wl = W[1, :, pl.ds(start, P_SIZE)]
-        y = dot(wh, XB[...])
-        r = y[:, :LANES] + y[:, LANES:] + dot(wl, XB[:, 0:LANES])
-        YA[2 * i] = r[0:SL]
-        YA[2 * i + 1] = r[SL:]
-
-        @pl.when(step > 0)
+        x = XB[:, 0:LANES]
+        y = dot(W[0, :, pl.ds(start, P_SIZE)], x) + dot(W[1, :, pl.ds(start, P_SIZE)], x)
+        r = y + pltpu.roll(y, 64, 1)
+        YB[2 * i] = jnp.where(left64, r[0:32], r[32:64])
+        YB[2 * i + 1] = jnp.where(left64, r[64:96], r[96:128])
+
+        @pl.when(i > 0)
         def _():
-            send_block(step - 1, YA, DA, s_ra, r_ra)
+            send_block(i - 1, YB, DB, s_rb, r_rb)
 
         return carry
 
-    lax.fori_loop(0, 8, rows_a, 0)
-    send_last(YA, DA, s_ra, r_ra)
+    lax.fori_loop(0, 8, rows_b, 0)
+    send_block(7, YB, DB, s_rb, r_rb)
 
     for i in range(3):
         wait_recv(VR, r_v, i)
@@ -344,42 +353,31 @@
             part = dot(hot, hi) + dot(hot, lo)
             SC[fp] = part if i == 0 else SC[fp] + part
 
-    def spread(x):
-        r = pltpu.roll(x, 64, 1)
-        return jnp.where(left64, x, r), jnp.where(left64, r, x)
-
-    def store_b(at, x):
-        hi, lo = halves(x)
-        keep = lanes_of(x.shape) < 64
-        XB[pl.ds(at, x.shape[0]), 0:LANES] = jnp.where(keep, hi.astype(F32), lo.astype(F32)).astype(BF16)
-
     for c, k in arrivals:
         s = 2 * c + k
-        wait_recv(XP, r_fb, s)
-        a, b = spread(XP[s])
-        store_b(pl.multiple_of(s * SL, SL), a)
-        store_b(pl.multiple_of(s * SL + 32, 32), b)
-    E[0:MATCH] = spread(XP[15])[1][32 - MATCH:]
-    E[MATCH:2 * MATCH] = spread(XP[0])[0][0:MATCH]
-    store_b(1024, exact_dot(C128[...], E[...]))
-
-    def rows_b(step, carry):
-        i = (zc + far_first(step) + 8) % 8
+        wait_recv(XF, r_fa, s)
+        store_a(pl.multiple_of(s * SL, SL), XF[s])
+    E[0:MATCH] = XF[15, SL - MATCH:]
+    E[MATCH:2 * MATCH] = XF[0, 0:MATCH]
+    store_a(1024, exact_dot(C128[...], E[...]))
+
+    def rows_a(i, carry):
         start = pl.multiple_of((7 - i) * LANES, LANES)
-        x = XB[:, 0:LANES]
-        y = dot(W[0, :, pl.ds(start, P_SIZE)], x) + dot(W[1, :, pl.ds(start, P_SIZE)], x)
-        r = y + pltpu.roll(y, 64, 1)
-        YB[2 * i] = jnp.where(left64, r[0:32], r[32:64])
-        YB[2 * i + 1] = jnp.where(left64, r[64:96], r[96:128])
-
-        @pl.when(step > 0)
+        wh = W[0, :, pl.ds(start, P_SIZE)]
+        wl = W[1, :, pl.ds(start, P_SIZE)]
+        y = dot(wh, XB[...])
+        r = y[:, :LANES] + y[:, LANES:] + dot(wl, XB[:, 0:LANES])
+        YA[2 * i] = r[0:SL]
+        YA[2 * i + 1] = r[SL:]
+
+        @pl.when(i > 0)
         def _():
-            send_block(step - 1, YB, DB, s_rb, r_rb)
+            send_block(i - 1, YA, DA, s_ra, r_ra)
 
         return carry
 
-    lax.fori_loop(0, 8, rows_b, 0)
-    send_last(YB, DB, s_rb, r_rb)
+    lax.fori_loop(0, 8, rows_a, 0)
+    send_block(7, YA, DA, s_ra, r_ra)
 
     pltpu.make_async_copy(HN, HN, r_h.at[0]).wait()
     pltpu.make_async_copy(HP, HP, r_h.at[1]).wait()
@@ -492,7 +490,7 @@
         vm((NF, SL, LANES), F32),
         dma((32,)), dma((20,)), dma((6,)),
         dma((15,)), dma((16,)), dma((15,)), dma((16,)),
-        dma((15,)), dma((16,)), dma((15,)), dma((16,)),
+        dma((16,)), dma((16,)), dma((16,)), dma((16,)),
         dma((3,)), dma((3,)), dma((3,)), dma((3,)), dma((3,)), dma((3,)),
         dma((2,)), dma((2,)),
     ]

time: 48.3 us -> 46.4 us (0.961)
  the two profiles are of different devices: /device:TPU:1 before, /device:TPU:65 now
where the time goes in v3:
time: 46.4 us; the launch traced here: 46.3 us
  Pallas kernels  45.7 us (98%)
  between operations  0.64 us (1%)
    pallas_call x1, Pallas kernels, per_device(): call(donor_counts, elastic, acoustic, el_media, ac_media, cont_matrix.T,...  44.4 us
    pallas_call x1, Pallas kernels, per_device(): pl.pallas_call(finish, out_shape=(jax.ShapeDtypeStruct(elastic.shape, F32...  1.25 us

profile of v3, /device:TPU:65, one launch (start us, length us, event | category | flops | bytes accessed | tf_op | source)
XLA Modules:
  0.0 46.3 jit_solution(14431305469109366602)
XLA Ops:
  0.6 44.4 %shard_map.131 = (f32[1,5,64,512]{3,2,1,0:T(8,128)S(1)}, f32[1,3,64,512]{3,2,1,0:T(8,128)S(1)}, f32[7,4,64,128]{3,2,1,0:T(8,128)S(1)}, f32[16,64,128]{2,1,0:T(8,128)S(1)}, f32[16,32,128]{2,1,0:T(8,128)S(1)}) custom-call(s32[1,1,1,4]{3,2,1,0:T(1,128)} %cnt.1, f32[1,5,64,512]{3,2,1,0:T(8,128)} %el.1, f32[1,3,64,512]{3,2,1,0:T(8,128)} %ac.1, ...), custom_call_target="tpu_custom_call" | custom-call | tf_op jit(solution)/shard_map/pallas_call | solution.py:508
  45.1 1.2 %shard_map.132 = (f32[1,5,64,512]{3,2,1,0:T(8,128)}, f32[1,3,64,512]{3,2,1,0:T(8,128)}) custom-call(f32[1,5,64,512]{3,2,1,0:T(8,128)S(1)} %get-tuple-element.7.bel, f32[1,3,64,512]{3,2,1,0:T(8,128)S(1)} %get-tuple-element.8.bac, f32[7,4,64,128]{3,2,1,0:T(8,128)S(1)} %get-tuple-element.9.CO, f32[16,64,128]{2,1,0:T(8,128)S(1)} %get-tuple-element.10.DA, ...), custom_call_target="tpu_custom_call" | custom-call | tf_op jit(solution)/shard_map/pallas_call | solution.py:512

commit v4 on v3

--- a/solution.py
+++ b/solution.py
@@ -146,11 +146,40 @@
         bot = F[t // 4, t % 4, 32:64]
         H[2 * c] = jnp.where(left64, top, pltpu.roll(bot, 64, 1))
         H[2 * c + 1] = jnp.where(left64, pltpu.roll(top, 64, 1), bot)
+
+    pl.semaphore_wait(barrier, len(partners))
+
+    order = [(dz, k) for dz in (4, 3, -3, 2, -2, 1, -1) for k in (0, 1)]
+    n_out = len(order)
+    other = 1 - core
+
+    def targets():
+        for i, (dz, k) in enumerate(order):
+            yield i, (zc + dz + 8) % 8, k
+        yield n_out, zc, other
+
+    def exchange(src_of, dst, send, recv):
+        copies = []
+        for i, c, k in targets():
+            copies.append(pltpu.make_async_remote_copy(
+                src_ref=src_of(c, k), dst_ref=dst.at[me], send_sem=send.at[i], recv_sem=recv.at[me],
+                device_id={"line": c * 2 + k}, device_id_type=MESH_ID))
+        own = pltpu.make_async_copy(src_of(zc, core), dst.at[me], recv.at[me])
+        for r in copies:
+            r.start()
+        own.start()
+        return copies
+
+    def full_tile(c, k):
+        t = 3 * c + 2 * k
+        return F.at[t // 4, t % 4]
+
+    fwd_b = exchange(lambda c, k: H.at[c * 2 + k], XP, s_fb, r_fb)
+    fwd_a = exchange(full_tile, XF, s_fa, r_fa)
+
     for f in range(6, 8):
         for q in range(NQ):
             loads[f, q].wait()
-
-    pl.semaphore_wait(barrier, len(partners))
 
     reqs = []
     for o in range(1, 4):
@@ -172,33 +201,6 @@
     halo_up.start()
     halo_down.start()
 
-    order = [(dz, k) for dz in (4, 3, -3, 2, -2, 1, -1) for k in (0, 1)]
-    n_out = len(order)
-    other = 1 - core
-
-    def targets():
-        for i, (dz, k) in enumerate(order):
-            yield i, (zc + dz + 8) % 8, k
-        yield n_out, zc, other
-
-    def exchange(src_of, dst, send, recv):
-        copies = []
-        for i, c, k in targets():
-            copies.append(pltpu.make_async_remote_copy(
-                src_ref=src_of(c, k), dst_ref=dst.at[me], send_sem=send.at[i], recv_sem=recv.at[me],
-                device_id={"line": c * 2 + k}, device_id_type=MESH_ID))
-        own = pltpu.make_async_copy(src_of(zc, core), dst.at[me], recv.at[me])
-        for r in copies:
-            r.start()
-        own.start()
-        return copies
-
-    def full_tile(c, k):
-        t = 3 * c + 2 * k
-        return F.at[t // 4, t % 4]
-
-    fwd_b = exchange(lambda c, k: H.at[c * 2 + k], XP, s_fb, r_fb)
-    fwd_a = exchange(full_tile, XF, s_fa, r_fa)
     for m in media:
         m.start()
 

time: 46.4 us -> 46.4 us (level)
  no operation moved by 1% of the time
where the time goes in v4:
time: 46.4 us; the launch traced here: 46.3 us
  Pallas kernels  45.7 us (98%)
  between operations  0.64 us (1%)
    pallas_call x1, Pallas kernels, per_device(): call(donor_counts, elastic, acoustic, el_media, ac_media, cont_matrix.T,...  44.4 us
    pallas_call x1, Pallas kernels, per_device(): pl.pallas_call(finish, out_shape=(jax.ShapeDtypeStruct(elastic.shape, F32...  1.25 us

profile of v4, /device:TPU:65, one launch (start us, length us, event | category | flops | bytes accessed | tf_op | source)
XLA Modules:
  0.0 46.3 jit_solution(12813422100876664476)
XLA Ops:
  0.6 44.4 %shard_map.131 = (f32[1,5,64,512]{3,2,1,0:T(8,128)S(1)}, f32[1,3,64,512]{3,2,1,0:T(8,128)S(1)}, f32[7,4,64,128]{3,2,1,0:T(8,128)S(1)}, f32[16,64,128]{2,1,0:T(8,128)S(1)}, f32[16,32,128]{2,1,0:T(8,128)S(1)}) custom-call(s32[1,1,1,4]{3,2,1,0:T(1,128)} %cnt.1, f32[1,5,64,512]{3,2,1,0:T(8,128)} %el.1, f32[1,3,64,512]{3,2,1,0:T(8,128)} %ac.1, ...), custom_call_target="tpu_custom_call" | custom-call | tf_op jit(solution)/shard_map/pallas_call | solution.py:510
  45.1 1.2 %shard_map.132 = (f32[1,5,64,512]{3,2,1,0:T(8,128)}, f32[1,3,64,512]{3,2,1,0:T(8,128)}) custom-call(f32[1,5,64,512]{3,2,1,0:T(8,128)S(1)} %get-tuple-element.7.bel, f32[1,3,64,512]{3,2,1,0:T(8,128)S(1)} %get-tuple-element.8.bac, f32[7,4,64,128]{3,2,1,0:T(8,128)S(1)} %get-tuple-element.9.CO, f32[16,64,128]{2,1,0:T(8,128)S(1)} %get-tuple-element.10.DA, ...), custom_call_target="tpu_custom_call" | custom-call | tf_op jit(solution)/shard_map/pallas_call | solution.py:514
